TPU v7x, 32 devices: a whole 2x2x4 slice. The times are simulated.
32 devices in a mesh: grp: 4 (over y, x), leaf: 8 (over z, core).
Axes of the slice: x: 2, y: 2, z: 4, core: 2. Of those that a mesh axis runs over, the one named last changes fastest.
Arguments:
- direction: bfloat16 [49152, 256], P(('grp', 'leaf')), may hold values from -6 to 6
- residual: bfloat16 [49152, 256], P(('grp', 'leaf')), may hold values from -6 to 6
- leaf_order: int32 [32, 1536], P(('grp', 'leaf')), may hold values from 0 to 1535, as said below
- diag_block: bfloat16 [32, 1536, 1536], P(('grp', 'leaf')), may hold values from -0.15625 to 0.15625
- up_basis: bfloat16 [32, 1536, 128], P(('grp', 'leaf')), may hold values from -0.15625 to 0.15625
- down_basis: bfloat16 [32, 1536, 128], P(('grp', 'leaf')), may hold values from -0.5 to 0.5
- leaf_ops: bfloat16 [3, 32, 128, 128], P(None, ('grp', 'leaf')), may hold values from -0.375 to 0.375
- inner_ops: bfloat16 [3, 24, 128, 128], P(None, 'grp'), may hold values from -0.375 to 0.375
- top_ops: bfloat16 [3, 6, 128, 128], replicated, may hold values from -0.375 to 0.375
- ridge_shift: float32 [1], replicated, may hold values from 0.5 to 2
Outputs:
- image: bfloat16 [49152, 256], P(('grp', 'leaf'))
- curvature_gram: float32 [256, 256], replicated
- residual_gram: float32 [256, 256], replicated
Inputs may be any that keep to these rules, and one draw needn't show every extreme that they name: Each row of leaf_order is a permutation of 0 to 1535.
All inputs are finite; a program needn't handle non-finite values.
Results may differ from a plain program's by a relative error of at most 0.022.
Values may be sent and summed in bfloat16 or wider, within the bound.
No kernel may reach another device: no remote copies, remote signals or barrier semaphores. Data moves between devices by JAX's collectives and lax.ppermute only.
A program may use at most 64 MiB of HBM per device.

v0:
```python
import jax
import jax.numpy as jnp
from jax import lax
from jax.sharding import PartitionSpec as P


def from_partner(block, axis, apart):
    count = lax.axis_size(axis)
    route = []
    for low in range(count):
        high = low | 1 << apart
        if high != low and high < count:
            route += [(low, high), (high, low)]
    return lax.ppermute(block, axis, route)


def lift_single(transfer, skeleton):
    return jnp.einsum("rs,rk->sk", transfer, skeleton, preferred_element_type=jnp.float32).astype(
        jnp.bfloat16
    )


def body(
    direction,
    residual,
    leaf_order,
    diag_block,
    up_basis,
    down_basis,
    leaf_ops,
    inner_ops,
    top_ops,
    ridge_shift,
):
    leaves_here = lax.axis_size("leaf")
    groups = lax.axis_size("grp")
    leaf_levels = leaves_here.bit_length() - 1
    group_levels = groups.bit_length() - 1
    total_levels = leaf_levels + group_levels
    my_leaf = lax.axis_index("leaf")
    my_group = lax.axis_index("grp")
    ordering = leaf_order[0]
    ordered = jnp.take(direction, ordering, axis=0)
    skeleton = jnp.einsum(
        "nr,nk->rk", up_basis[0], ordered, preferred_element_type=jnp.float32
    ).astype(jnp.bfloat16)

    def inner_offset(height):
        return sum((leaves_here >> section for section in range(1, height)))

    def top_offset(upper_level):
        return sum((groups >> section for section in range(upper_level)))

    def path_operators(height):
        if height == 0:
            return leaf_ops[:, 0]
        if height < leaf_levels:
            return lax.dynamic_index_in_dim(
                inner_ops, inner_offset(height) + (my_leaf >> height), 1, keepdims=False
            )
        upper_level = height - leaf_levels
        return lax.dynamic_index_in_dim(
            top_ops, top_offset(upper_level) + (my_group >> upper_level), 1, keepdims=False
        )

    contrib = lift_single(leaf_ops[0, 0], skeleton)
    siblings = []
    for bit_index in range(leaf_levels):
        other_skeleton, other_contrib = from_partner((skeleton, contrib), "leaf", bit_index)
        siblings.append(other_skeleton)
        skeleton = (contrib.astype(jnp.float32) + other_contrib.astype(jnp.float32)).astype(
            jnp.bfloat16
        )
        contrib = lift_single(path_operators(bit_index + 1)[0], skeleton)
    for bit_index in range(group_levels):
        other_skeleton, other_contrib = from_partner((skeleton, contrib), "grp", bit_index)
        siblings.append(other_skeleton)
        if bit_index + 1 < group_levels:
            skeleton = (contrib.astype(jnp.float32) + other_contrib.astype(jnp.float32)).astype(
                jnp.bfloat16
            )
            contrib = lift_single(path_operators(leaf_levels + bit_index + 1)[0], skeleton)
    coarse = jnp.zeros((up_basis.shape[2], direction.shape[1]), jnp.bfloat16)
    for height in reversed(range(total_levels)):
        operators = path_operators(height)
        coupled = jnp.dot(operators[2], siblings[height], preferred_element_type=jnp.float32)
        passed = jnp.dot(operators[1], coarse, preferred_element_type=jnp.float32)
        coarse = (coupled + passed).astype(jnp.bfloat16)
    local = jnp.dot(diag_block[0], ordered, preferred_element_type=jnp.float32)
    local = local + jnp.dot(down_basis[0], coarse, preferred_element_type=jnp.float32)
    restored = jnp.zeros(local.shape, jnp.float32).at[ordering].set(local)
    image = (restored + ridge_shift[0] * direction.astype(jnp.float32)).astype(jnp.bfloat16)
    curvature_part = jnp.einsum("nk,nm->km", direction, image, preferred_element_type=jnp.float32)
    correlation_part = jnp.einsum("nk,nm->km", residual, image, preferred_element_type=jnp.float32)
    curvature, correlation = lax.psum((curvature_part, correlation_part), ("grp", "leaf"))
    points_total = direction.shape[0] * leaves_here * groups
    return (image, curvature / points_total, correlation / points_total)


def solution(mesh):
    return jax.shard_map(
        body,
        mesh=mesh,
        in_specs=(
            P(("grp", "leaf"), None),
            P(("grp", "leaf"), None),
            P(("grp", "leaf"), None),
            P(("grp", "leaf"), None, None),
            P(("grp", "leaf"), None, None),
            P(("grp", "leaf"), None, None),
            P(None, ("grp", "leaf"), None, None),
            P(None, "grp", None, None),
            P(),
            P(),
        ),
        out_specs=(P(("grp", "leaf"), None), P(), P()),
        check_vma=False,
    )
```

profile of v0, /device:TPU:0, one launch (start us, length us, event | category | flops | bytes accessed | tf_op | source)
XLA Modules:
  0.0 201.7 jit_solution(530703202432133354)
XLA Ops:
  7.2 0.0 copy-start
  7.2 0.0 all-reduce.3.cloned.1.call-start
  7.2 0.8 fusion.27
  8.0 0.7 reduce.1
  8.8 0.0 copy-start.5
  8.8 4.9 %gather_fusion = bf16[1536,256]{1,0:T(8,128)(2,1)S(1)} fusion(bf16[1536,256]{1,0:T(8,128)(2,1)} %param.10, s32[2048]{0:T(1024)S(1)} %pad_clamp_fusion), kind=kCustom, calls=%fused_computation | custom fusion | bytes 1579008 | tf_op jit(solution)/shard_map/jit(_take)/gather | solution.py:43
  13.7 0.0 copy-start.4
  13.7 0.7 convolution_convert_fusion
  14.4 0.2 copy-done.4
  14.6 0.1 fusion.8
  14.8 0.6 collective-permute-start.1
  15.3 0.9 collective-permute-done.1
  16.2 1.0 convolution_convert_fusion.3
  17.2 3.0 %collective-permute-start.3 = (bf16[128,256]{1,0:T(8,128)(2,1)S(1)}, bf16[128,256]{1,0:T(8,128)(2,1)S(1)}, u32[]{:S(2)}, u32[]{:S(2)}) collective-permute-start(bf16[128,256]{1,0:T(8,128)(2,1)S(1)} %convolution_convert_fusion.3), channel_id=1, source_target_pairs={{0,2},{2,0},{1,3},{3,1},{4,6},{6,4},{5,7},{7,5},{8,10},{10,8},{9,1... | collective-permute-start | bytes 196616 | tf_op jit(solution)/shard_map/ppermute | solution.py:14
  20.2 2.4 %collective-permute-done.3 = bf16[128,256]{1,0:T(8,128)(2,1)S(1)} collective-permute-done((bf16[128,256]{1,0:T(8,128)(2,1)S(1)}, bf16[128,256]{1,0:T(8,128)(2,1)S(1)}, u32[]{:S(2)}, u32[]{:S(2)}) %collective-permute-start.3) | collective-permute-done | bytes 65568 | tf_op jit(solution)/shard_map/ppermute | solution.py:14
  22.6 1.0 convolution_convert_fusion.2
  23.6 2.9 %collective-permute-start.5 = (bf16[128,256]{1,0:T(8,128)(2,1)S(1)}, bf16[128,256]{1,0:T(8,128)(2,1)S(1)}, u32[]{:S(2)}, u32[]{:S(2)}) collective-permute-start(bf16[128,256]{1,0:T(8,128)(2,1)S(1)} %convolution_convert_fusion.2), channel_id=1, source_target_pairs={{0,4},{4,0},{1,5},{5,1},{2,6},{6,2},{3,7},{7,3},{8,12},{12,8},{9,1... | collective-permute-start | bytes 196616 | tf_op jit(solution)/shard_map/ppermute | solution.py:14
  26.5 0.0 collective-permute-start
  26.5 2.3 %collective-permute-done.5 = bf16[128,256]{1,0:T(8,128)(2,1)S(1)} collective-permute-done((bf16[128,256]{1,0:T(8,128)(2,1)S(1)}, bf16[128,256]{1,0:T(8,128)(2,1)S(1)}, u32[]{:S(2)}, u32[]{:S(2)}) %collective-permute-start.5) | collective-permute-done | bytes 65568 | tf_op jit(solution)/shard_map/ppermute | solution.py:14
  28.9 1.0 convolution_convert_fusion.1
  29.8 1.8 collective-permute-start.7
  31.6 5.3 %fusion = f32[256,1536]{1,0:T(8,128)} fusion(bf16[1,1536,1536]{2,1,0:T(8,128)(2,1)} %param.13, bf16[1536,256]{1,0:T(8,128)(2,1)S(1)} %gather_fusion, pred[1536]{0:T(1024)(128)(4,1)S(1)} %compare_and_fusion), kind=kOutput, calls=%fused_computation.2 | convolution fusion | flops 1208352768 | bytes 7079424 | tf_op jit(solution)/shard_map/dot_general | solution.py:89
  37.6 0.0 collective-permute-done.7
  37.6 1.6 collective-permute-start.8
  39.2 0.9 fusion.17
  40.1 1.6 collective-permute-start.2
  41.7 3.2 %collective-permute-start.4 = (bf16[128,256]{1,0:T(8,128)(2,1)S(1)}, bf16[128,256]{1,0:T(8,128)(2,1)S(1)}, u32[]{:S(2)}, u32[]{:S(2)}) collective-permute-start(bf16[128,256]{1,0:T(8,128)(2,1)S(1)} %add_convert_fusion.3), channel_id=1, source_target_pairs={{0,4},{4,0},{1,5},{5,1},{2,6},{6,2},{3,7},{7,3},{8,12},{12,8},{9,1... | collective-permute-start | bytes 196616 | tf_op jit(solution)/shard_map/ppermute | solution.py:14
  44.8 0.5 collective-permute-start.6
  45.4 0.0 collective-permute-done.8
  45.4 1.1 fusion.9
  46.5 2.6 %collective-permute-done.6 = bf16[128,256]{1,0:T(8,128)(2,1)S(1)} collective-permute-done((bf16[128,256]{1,0:T(8,128)(2,1)S(1)}, bf16[128,256]{1,0:T(8,128)(2,1)S(1)}, u32[]{:S(2)}, u32[]{:S(2)}) %collective-permute-start.6) | collective-permute-done | bytes 65568 | tf_op jit(solution)/shard_map/ppermute | solution.py:14
  49.1 1.1 fusion.10
  50.2 0.0 collective-permute-done.4
  50.2 1.1 fusion.11
  51.3 0.0 collective-permute-done.2
  51.3 1.1 fusion.12
  52.5 1.9 fusion.2
  54.4 1.6 copy.16
  56.0 7.8 %scatter_custom_fusion = f32[1536,256]{1,0:T(8,128)S(1)} fusion(s32[1536]{0:T(1024)S(1)} %fusion.27, f32[1536,256]{1,0:T(8,128)} %copy.16, f32[]{:T(128)} %constant.47.clone.1), kind=kCustom, calls=%fused_computation.29 | custom fusion | bytes 1573376 | tf_op jit(solution)/shard_map/scatter | solution.py:91
  63.8 0.2 add_convert_fusion
  64.0 0.0 copy-start.2
  64.1 1.1 convolution_bitcast_fusion.1
  65.2 1.1 convolution_bitcast_fusion
  66.3 0.0 all-reduce.3.cloned.1.call-update
  66.3 125.8 %all-reduce.3.cloned.1.call-done = (f32[256,256]{0,1:T(8,128)}, f32[256,256]{0,1:T(8,128)}) async-done(((f32[256,256]{0,1:T(8,128)}, f32[256,256]{0,1:T(8,128)}), (f32[256,256]{0,1:T(8,128)}, f32[256,256]{0,1:T(8,128)})) %all-reduce.3.cloned.1.call-update) | async-done | bytes 524304 | tf_op jit(solution)/shard_map/psum | solution.py:95
  192.1 1.1 broadcast_multiply_fusion
  193.2 0.8 copy.17
  194.0 0.8 copy.18
  (14 shorter events, 0.1 us)
Async XLA Ops:
  7.2 58.0 %copy-start = (bf16[1536,256]{1,0:T(8,128)(2,1)S(1)}, bf16[1536,256]{1,0:T(8,128)(2,1)}, u32[]{:S(2)}) copy-start(bf16[1536,256]{1,0:T(8,128)(2,1)} %param.11) | copy-start | bytes 2359300
  7.2 184.9 %all-reduce.3.cloned.1.call-start = ((), (), s32[]{:S(2)}) async-start(), calls=%async_computation | async-start | bytes 1048576 | tf_op jit(solution)/shard_map/psum | solution.py:95
  8.8 5.0 %copy-start.5 = (bf16[1,1536,128]{2,1,0:T(8,128)(2,1)S(1)}, bf16[1,1536,128]{2,1,0:T(8,128)(2,1)}, u32[]{:S(2)}) copy-start(bf16[1,1536,128]{2,1,0:T(8,128)(2,1)} %param.14) | copy-start | bytes 1179652
  13.7 0.9 copy-start.4
  14.8 1.5 collective-permute-start.1
  17.2 5.4 %collective-permute-start.3 = (bf16[128,256]{1,0:T(8,128)(2,1)S(1)}, bf16[128,256]{1,0:T(8,128)(2,1)S(1)}, u32[]{:S(2)}, u32[]{:S(2)}) collective-permute-start(bf16[128,256]{1,0:T(8,128)(2,1)S(1)} %convolution_convert_fusion.3), channel_id=1, source_target_pairs={{0,2},{2,0},{1,3},{3,1},{4,6},{6,4},{5,7},{7,5},{8,10},{10,8},{9,1... | collective-permute-start | bytes 196616 | tf_op jit(solution)/shard_map/ppermute | solution.py:14
  23.6 5.3 %collective-permute-start.5 = (bf16[128,256]{1,0:T(8,128)(2,1)S(1)}, bf16[128,256]{1,0:T(8,128)(2,1)S(1)}, u32[]{:S(2)}, u32[]{:S(2)}) collective-permute-start(bf16[128,256]{1,0:T(8,128)(2,1)S(1)} %convolution_convert_fusion.2), channel_id=1, source_target_pairs={{0,4},{4,0},{1,5},{5,1},{2,6},{6,2},{3,7},{7,3},{8,12},{12,8},{9,1... | collective-permute-start | bytes 196616 | tf_op jit(solution)/shard_map/ppermute | solution.py:14
  26.5 25.9 %collective-permute-start = (bf16[128,256]{0,1:T(8,128)(2,1)S(1)}, bf16[128,256]{0,1:T(8,128)(2,1)S(1)}, u32[]{:S(2)}, u32[]{:S(2)}) collective-permute-start(bf16[128,256]{0,1:T(8,128)(2,1)S(1)} %bitcast.82), channel_id=1, source_target_pairs={{0,1},{1,0},{2,3},{3,2},{4,5},{5,4},{6,7},{7,6},{8,9},{9,8},{10,11... | collective-permute-start | bytes 196616 | tf_op jit(solution)/shard_map/ppermute | solution.py:14
  29.8 7.8 %collective-permute-start.7 = (bf16[128,256]{1,0:T(8,128)(2,1)S(1)}, bf16[128,256]{1,0:T(8,128)(2,1)S(1)}, u32[]{:S(2)}, u32[]{:S(2)}) collective-permute-start(bf16[128,256]{1,0:T(8,128)(2,1)S(1)} %convolution_convert_fusion.1), channel_id=1, source_target_pairs={{0,8},{8,0},{16,24},{24,16},{1,9},{9,1},{17,25},{25,17},{2,10},{10... | collective-permute-start | bytes 196616 | tf_op jit(solution)/shard_map/ppermute | solution.py:14
  36.9 15.6 %copy-start.3 = (bf16[1,1536,128]{2,1,0:T(8,128)(2,1)S(1)}, bf16[1,1536,128]{2,1,0:T(8,128)(2,1)}, u32[]{:S(2)}) copy-start(bf16[1,1536,128]{2,1,0:T(8,128)(2,1)} %param.15) | copy-start | bytes 1179652
  37.6 7.8 %collective-permute-start.8 = (bf16[128,256]{1,0:T(8,128)(2,1)S(1)}, bf16[128,256]{1,0:T(8,128)(2,1)S(1)}, u32[]{:S(2)}, u32[]{:S(2)}) collective-permute-start(bf16[128,256]{1,0:T(8,128)(2,1)S(1)} %add_convert_fusion.1), channel_id=1, source_target_pairs={{0,16},{16,0},{8,24},{24,8},{1,17},{17,1},{9,25},{25,9},{2,18},{18... | collective-permute-start | bytes 196616 | tf_op jit(solution)/shard_map/ppermute | solution.py:14
  40.1 11.2 %collective-permute-start.2 = (bf16[128,256]{0,1:T(8,128)(2,1)S(1)}, bf16[128,256]{0,1:T(8,128)(2,1)S(1)}, u32[]{:S(2)}, u32[]{:S(2)}) collective-permute-start(bf16[128,256]{0,1:T(8,128)(2,1)S(1)} %add_convert_fusion.4), channel_id=1, source_target_pairs={{0,2},{2,0},{1,3},{3,1},{4,6},{6,4},{5,7},{7,5},{8,10},{10,8},{9,1... | collective-permute-start | bytes 196616 | tf_op jit(solution)/shard_map/ppermute | solution.py:14
  41.7 8.5 %collective-permute-start.4 = (bf16[128,256]{1,0:T(8,128)(2,1)S(1)}, bf16[128,256]{1,0:T(8,128)(2,1)S(1)}, u32[]{:S(2)}, u32[]{:S(2)}) collective-permute-start(bf16[128,256]{1,0:T(8,128)(2,1)S(1)} %add_convert_fusion.3), channel_id=1, source_target_pairs={{0,4},{4,0},{1,5},{5,1},{2,6},{6,2},{3,7},{7,3},{8,12},{12,8},{9,1... | collective-permute-start | bytes 196616 | tf_op jit(solution)/shard_map/ppermute | solution.py:14
  44.8 4.3 %collective-permute-start.6 = (bf16[128,256]{1,0:T(8,128)(2,1)S(1)}, bf16[128,256]{1,0:T(8,128)(2,1)S(1)}, u32[]{:S(2)}, u32[]{:S(2)}) collective-permute-start(bf16[128,256]{1,0:T(8,128)(2,1)S(1)} %add_convert_fusion.2), channel_id=1, source_target_pairs={{0,8},{8,0},{16,24},{24,16},{1,9},{9,1},{17,25},{25,17},{2,10},{10... | collective-permute-start | bytes 196616 | tf_op jit(solution)/shard_map/ppermute | solution.py:14
  56.0 7.8 %copy-start.1 = (bf16[1536,256]{1,0:T(8,128)(2,1)S(1)}, bf16[1536,256]{1,0:T(8,128)(2,1)}, u32[]{:S(2)}) copy-start(bf16[1536,256]{1,0:T(8,128)(2,1)} %param.10) | copy-start | bytes 2359300
  64.0 1.1 copy-start.2
Sparse Core Ops, SparseCore 0:
  66.4 125.6 all-reduce.2
where the time goes:
time: 203 us; the launch traced here: 202 us
  waiting for transfers between devices  134 us (66%)
  matrix products  18.4 us (9%)
  local copies, waits for them, and re-layouts  16.2 us (8%)
  starting transfers between devices  15.2 us (7%)
  between operations  14.9 us (7%)
  other arithmetic  2.88 us (1%)
    psum x1, waiting for transfers between devices, body(): lax.psum((curvature_part, correlation_part), ('grp', 'leaf'))  126 us
    ppermute x9, starting transfers between devices, from_partner(): return lax.ppermute(block, axis, route)  15.1 us
    ppermute x9, waiting for transfers between devices, from_partner(): return lax.ppermute(block, axis, route)  8.29 us
    scatter x1, local copies, waits for them, and re-layouts, body(): restored = jnp.zeros(local.shape, jnp.float32).at[ordering].set(local)  7.8 us
    dot_general x5, matrix products, body(): passed = jnp.dot(operators[1], coarse, preferred_element_type=jnp.float32)  5.26 us
    dot_general x1, matrix products, body(): local = jnp.dot(diag_block[0], ordered, preferred_element_type=jnp.float32)  5.26 us
    gather x1, local copies, waits for them, and re-layouts, body(): ordered = jnp.take(direction, ordering, axis=0)  4.93 us
  transfers between devices with their start and end apart: 10, of which 5 were waited for; matrix products, arithmetic and copies ran while one was open for 6% of the time, Pallas kernels for 0%

commit v1 on v0

--- a/solution.py
+++ b/solution.py
@@ -2,6 +2,11 @@
 import jax.numpy as jnp
 from jax import lax
 from jax.sharding import PartitionSpec as P
+
+
+def one_after_other(array, first, second):
+    partial = lax.psum(array, first)
+    return lax.psum(partial, second)
 
 
 def from_partner(block, axis, apart):
@@ -92,7 +97,7 @@
     image = (restored + ridge_shift[0] * direction.astype(jnp.float32)).astype(jnp.bfloat16)
     curvature_part = jnp.einsum("nk,nm->km", direction, image, preferred_element_type=jnp.float32)
     correlation_part = jnp.einsum("nk,nm->km", residual, image, preferred_element_type=jnp.float32)
-    curvature, correlation = lax.psum((curvature_part, correlation_part), ("grp", "leaf"))
+    curvature, correlation = one_after_other((curvature_part, correlation_part), "leaf", "grp")
     points_total = direction.shape[0] * leaves_here * groups
     return (image, curvature / points_total, correlation / points_total)
 

time: 203 us -> 177 us (0.87)
  waiting for transfers between devices: 134 us -> 109 us
    psum x1 -> x2, waiting for transfers between devices: 126 us -> 101 us  [the longest x1 53 us: one_after_other(): partial = lax.psum(array, first)]
  transfers between devices with their start and end apart: 10 -> 11, of which waited for: 5 -> 6; matrix products, arithmetic and copies ran while one was open for 6% -> 7% of each run, Pallas kernels for 0% -> 0%
where the time goes in v1:
time: 177 us
  waiting for transfers between devices  109 us (62%)
  matrix products  18.4 us (10%)
  local copies, waits for them, and re-layouts  16.3 us (9%)
  starting transfers between devices  15.2 us (9%)
  between operations  14.9 us (8%)
  other arithmetic  2.88 us (2%)
    psum x1, waiting for transfers between devices, one_after_other(): partial = lax.psum(array, first)  53 us
    psum x1, waiting for transfers between devices, one_after_other(): return lax.psum(partial, second)  47.5 us
    ppermute x9, starting transfers between devices, from_partner(): return lax.ppermute(block, axis, route)  15.1 us
    ppermute x9, waiting for transfers between devices, from_partner(): return lax.ppermute(block, axis, route)  8.29 us
    scatter x1, local copies, waits for them, and re-layouts, body(): restored = jnp.zeros(local.shape, jnp.float32).at[ordering].set(local)  7.8 us
    dot_general x1, matrix products, body(): local = jnp.dot(diag_block[0], ordered, preferred_element_type=jnp.float32)  5.27 us
    dot_general x5, matrix products, body(): passed = jnp.dot(operators[1], coarse, preferred_element_type=jnp.float32)  5.26 us
    gather x1, local copies, waits for them, and re-layouts, body(): ordered = jnp.take(direction, ordering, axis=0)  4.93 us
  transfers between devices with their start and end apart: 11, of which 6 were waited for; matrix products, arithmetic and copies ran while one was open for 7% of the time, Pallas kernels for 0%

profile of v1, /device:TPU:0, one launch (start us, length us, event | category | flops | bytes accessed | tf_op | source)
XLA Modules:
  0.0 176.5 jit_solution(14040519780217156872)
XLA Ops:
  7.2 0.0 copy-start
  7.2 0.0 all-reduce.5.cloned.1.call-start
  7.2 0.8 fusion.27
  8.0 0.7 reduce.1
  8.8 0.0 copy-start.5
  8.8 4.9 %gather_fusion = bf16[1536,256]{1,0:T(8,128)(2,1)S(1)} fusion(bf16[1536,256]{1,0:T(8,128)(2,1)} %param.10, s32[2048]{0:T(1024)S(1)} %pad_clamp_fusion), kind=kCustom, calls=%fused_computation | custom fusion | bytes 1579008 | tf_op jit(solution)/shard_map/jit(_take)/gather | solution.py:48
  13.7 0.0 copy-start.4
  13.7 0.7 convolution_convert_fusion
  14.4 0.2 copy-done.4
  14.6 0.1 fusion.8
  14.8 0.6 collective-permute-start.1
  15.3 0.9 collective-permute-done.1
  16.2 1.0 convolution_convert_fusion.3
  17.2 3.0 %collective-permute-start.3 = (bf16[128,256]{1,0:T(8,128)(2,1)S(1)}, bf16[128,256]{1,0:T(8,128)(2,1)S(1)}, u32[]{:S(2)}, u32[]{:S(2)}) collective-permute-start(bf16[128,256]{1,0:T(8,128)(2,1)S(1)} %convolution_convert_fusion.3), channel_id=1, source_target_pairs={{0,2},{2,0},{1,3},{3,1},{4,6},{6,4},{5,7},{7,5},{8,10},{10,8},{9,1... | collective-permute-start | bytes 196616 | tf_op jit(solution)/shard_map/ppermute | solution.py:19
  20.2 2.4 %collective-permute-done.3 = bf16[128,256]{1,0:T(8,128)(2,1)S(1)} collective-permute-done((bf16[128,256]{1,0:T(8,128)(2,1)S(1)}, bf16[128,256]{1,0:T(8,128)(2,1)S(1)}, u32[]{:S(2)}, u32[]{:S(2)}) %collective-permute-start.3) | collective-permute-done | bytes 65568 | tf_op jit(solution)/shard_map/ppermute | solution.py:19
  22.6 1.0 convolution_convert_fusion.2
  23.6 2.9 %collective-permute-start.5 = (bf16[128,256]{1,0:T(8,128)(2,1)S(1)}, bf16[128,256]{1,0:T(8,128)(2,1)S(1)}, u32[]{:S(2)}, u32[]{:S(2)}) collective-permute-start(bf16[128,256]{1,0:T(8,128)(2,1)S(1)} %convolution_convert_fusion.2), channel_id=1, source_target_pairs={{0,4},{4,0},{1,5},{5,1},{2,6},{6,2},{3,7},{7,3},{8,12},{12,8},{9,1... | collective-permute-start | bytes 196616 | tf_op jit(solution)/shard_map/ppermute | solution.py:19
  26.5 2.3 %collective-permute-done.5 = bf16[128,256]{1,0:T(8,128)(2,1)S(1)} collective-permute-done((bf16[128,256]{1,0:T(8,128)(2,1)S(1)}, bf16[128,256]{1,0:T(8,128)(2,1)S(1)}, u32[]{:S(2)}, u32[]{:S(2)}) %collective-permute-start.5) | collective-permute-done | bytes 65568 | tf_op jit(solution)/shard_map/ppermute | solution.py:19
  28.9 1.0 convolution_convert_fusion.1
  29.8 1.8 %collective-permute-start.7 = (bf16[128,256]{1,0:T(8,128)(2,1)S(1)}, bf16[128,256]{1,0:T(8,128)(2,1)S(1)}, u32[]{:S(2)}, u32[]{:S(2)}) collective-permute-start(bf16[128,256]{1,0:T(8,128)(2,1)S(1)} %convolution_convert_fusion.1), channel_id=1, source_target_pairs={{0,8},{8,0},{16,24},{24,16},{1,9},{9,1},{17,25},{25,17},{2,10},{10... | collective-permute-start | bytes 196616 | tf_op jit(solution)/shard_map/ppermute | solution.py:19
  31.6 5.3 %fusion = f32[256,1536]{1,0:T(8,128)} fusion(bf16[1,1536,1536]{2,1,0:T(8,128)(2,1)} %param.13, bf16[1536,256]{1,0:T(8,128)(2,1)S(1)} %gather_fusion, pred[1536]{0:T(1024)(128)(4,1)S(1)} %compare_and_fusion), kind=kOutput, calls=%fused_computation.2 | convolution fusion | flops 1208352768 | bytes 7079424 | tf_op jit(solution)/shard_map/dot_general | solution.py:94
  37.6 0.0 collective-permute-done.7
  37.6 1.6 collective-permute-start.8
  39.2 0.9 fusion.17
  40.1 1.6 collective-permute-start.2
  41.7 3.2 %collective-permute-start.4 = (bf16[128,256]{1,0:T(8,128)(2,1)S(1)}, bf16[128,256]{1,0:T(8,128)(2,1)S(1)}, u32[]{:S(2)}, u32[]{:S(2)}) collective-permute-start(bf16[128,256]{1,0:T(8,128)(2,1)S(1)} %add_convert_fusion.3), channel_id=1, source_target_pairs={{0,4},{4,0},{1,5},{5,1},{2,6},{6,2},{3,7},{7,3},{8,12},{12,8},{9,1... | collective-permute-start | bytes 196616 | tf_op jit(solution)/shard_map/ppermute | solution.py:19
  44.9 0.5 collective-permute-start.6
  45.4 1.1 fusion.9
  46.5 2.6 %collective-permute-done.6 = bf16[128,256]{1,0:T(8,128)(2,1)S(1)} collective-permute-done((bf16[128,256]{1,0:T(8,128)(2,1)S(1)}, bf16[128,256]{1,0:T(8,128)(2,1)S(1)}, u32[]{:S(2)}, u32[]{:S(2)}) %collective-permute-start.6) | collective-permute-done | bytes 65568 | tf_op jit(solution)/shard_map/ppermute | solution.py:19
  49.1 1.1 fusion.10
  50.2 0.0 collective-permute-done.4
  50.2 1.1 fusion.11
  51.3 1.1 fusion.12
  52.5 1.9 %fusion.2 = f32[1536,256]{0,1:T(8,128)S(1)} fusion(f32[256,1536]{1,0:T(8,128)} %fusion, f32[256,128]{1,0:T(8,128)S(1)} %fusion.12, bf16[128,256]{0,1:T(8,128)(2,1)S(1)} %collective-permute-done, bf16[1,1536,128]{2,1,0:T(8,128)(2,1)S(1)} %copy-done.3, bf16[3,1,128,128]{3,2,1,0:T(8,128)(2,1)S(1)} %copy-done.4), kind=kOutput, calls=%fused_computation.5 | convolution fusion | flops 109510656 | bytes 3768320 | tf_op jit(solution)/shard_map/dot_general | solution.py:95
  54.4 1.6 copy.16
  56.0 7.8 %scatter_custom_fusion = f32[1536,256]{1,0:T(8,128)S(1)} fusion(s32[1536]{0:T(1024)S(1)} %fusion.27, f32[1536,256]{1,0:T(8,128)} %copy.16, f32[]{:T(128)} %constant.47.clone.1), kind=kCustom, calls=%fused_computation.29 | custom fusion | bytes 1573376 | tf_op jit(solution)/shard_map/scatter | solution.py:96
  63.9 0.2 add_convert_fusion
  64.1 0.0 copy-start.2
  64.1 1.1 convolution_bitcast_fusion.1
  65.2 1.1 convolution_bitcast_fusion
  66.3 0.0 all-reduce.5.cloned.1.call-update
  66.3 0.0 all-reduce.7.cloned.1.call-start
  66.4 53.0 %all-reduce.5.cloned.1.call-done = (f32[256,256]{0,1:T(8,128)}, f32[256,256]{0,1:T(8,128)}) async-done(((f32[256,256]{0,1:T(8,128)}, f32[256,256]{0,1:T(8,128)}), (f32[256,256]{0,1:T(8,128)}, f32[256,256]{0,1:T(8,128)})) %all-reduce.5.cloned.1.call-update) | async-done | bytes 524304 | tf_op jit(solution)/shard_map/psum | solution.py:8
  119.4 0.0 all-reduce.7.cloned.1.call-update
  119.5 47.5 %all-reduce.7.cloned.1.call-done = (f32[256,256]{0,1:T(8,128)}, f32[256,256]{0,1:T(8,128)}) async-done(((f32[256,256]{0,1:T(8,128)}, f32[256,256]{0,1:T(8,128)}), (f32[256,256]{0,1:T(8,128)}, f32[256,256]{0,1:T(8,128)})) %all-reduce.7.cloned.1.call-update) | async-done | bytes 524304 | tf_op jit(solution)/shard_map/psum | solution.py:9
  166.9 1.1 broadcast_multiply_fusion
  168.0 0.8 copy.17
  168.8 0.8 copy.18
  (17 shorter events, 0.1 us)
Async XLA Ops:
  7.2 58.0 %copy-start = (bf16[1536,256]{1,0:T(8,128)(2,1)S(1)}, bf16[1536,256]{1,0:T(8,128)(2,1)}, u32[]{:S(2)}) copy-start(bf16[1536,256]{1,0:T(8,128)(2,1)} %param.11) | copy-start | bytes 2359300
  7.2 112.3 %all-reduce.5.cloned.1.call-start = ((), (), s32[]{:S(2)}) async-start(), calls=%async_computation | async-start | bytes 1048576 | tf_op jit(solution)/shard_map/psum | solution.py:8
  8.8 5.0 %copy-start.5 = (bf16[1,1536,128]{2,1,0:T(8,128)(2,1)S(1)}, bf16[1,1536,128]{2,1,0:T(8,128)(2,1)}, u32[]{:S(2)}) copy-start(bf16[1,1536,128]{2,1,0:T(8,128)(2,1)} %param.14) | copy-start | bytes 1179652
  13.7 0.9 copy-start.4
  14.8 1.5 collective-permute-start.1
  17.2 5.4 %collective-permute-start.3 = (bf16[128,256]{1,0:T(8,128)(2,1)S(1)}, bf16[128,256]{1,0:T(8,128)(2,1)S(1)}, u32[]{:S(2)}, u32[]{:S(2)}) collective-permute-start(bf16[128,256]{1,0:T(8,128)(2,1)S(1)} %convolution_convert_fusion.3), channel_id=1, source_target_pairs={{0,2},{2,0},{1,3},{3,1},{4,6},{6,4},{5,7},{7,5},{8,10},{10,8},{9,1... | collective-permute-start | bytes 196616 | tf_op jit(solution)/shard_map/ppermute | solution.py:19
  23.6 5.3 %collective-permute-start.5 = (bf16[128,256]{1,0:T(8,128)(2,1)S(1)}, bf16[128,256]{1,0:T(8,128)(2,1)S(1)}, u32[]{:S(2)}, u32[]{:S(2)}) collective-permute-start(bf16[128,256]{1,0:T(8,128)(2,1)S(1)} %convolution_convert_fusion.2), channel_id=1, source_target_pairs={{0,4},{4,0},{1,5},{5,1},{2,6},{6,2},{3,7},{7,3},{8,12},{12,8},{9,1... | collective-permute-start | bytes 196616 | tf_op jit(solution)/shard_map/ppermute | solution.py:19
  26.5 25.9 %collective-permute-start = (bf16[128,256]{0,1:T(8,128)(2,1)S(1)}, bf16[128,256]{0,1:T(8,128)(2,1)S(1)}, u32[]{:S(2)}, u32[]{:S(2)}) collective-permute-start(bf16[128,256]{0,1:T(8,128)(2,1)S(1)} %bitcast.82), channel_id=1, source_target_pairs={{0,1},{1,0},{2,3},{3,2},{4,5},{5,4},{6,7},{7,6},{8,9},{9,8},{10,11... | collective-permute-start | bytes 196616 | tf_op jit(solution)/shard_map/ppermute | solution.py:19
  29.8 7.8 %collective-permute-start.7 = (bf16[128,256]{1,0:T(8,128)(2,1)S(1)}, bf16[128,256]{1,0:T(8,128)(2,1)S(1)}, u32[]{:S(2)}, u32[]{:S(2)}) collective-permute-start(bf16[128,256]{1,0:T(8,128)(2,1)S(1)} %convolution_convert_fusion.1), channel_id=1, source_target_pairs={{0,8},{8,0},{16,24},{24,16},{1,9},{9,1},{17,25},{25,17},{2,10},{10... | collective-permute-start | bytes 196616 | tf_op jit(solution)/shard_map/ppermute | solution.py:19
  36.9 15.6 %copy-start.3 = (bf16[1,1536,128]{2,1,0:T(8,128)(2,1)S(1)}, bf16[1,1536,128]{2,1,0:T(8,128)(2,1)}, u32[]{:S(2)}) copy-start(bf16[1,1536,128]{2,1,0:T(8,128)(2,1)} %param.15) | copy-start | bytes 1179652
  37.6 7.8 %collective-permute-start.8 = (bf16[128,256]{1,0:T(8,128)(2,1)S(1)}, bf16[128,256]{1,0:T(8,128)(2,1)S(1)}, u32[]{:S(2)}, u32[]{:S(2)}) collective-permute-start(bf16[128,256]{1,0:T(8,128)(2,1)S(1)} %add_convert_fusion.1), channel_id=1, source_target_pairs={{0,16},{16,0},{8,24},{24,8},{1,17},{17,1},{9,25},{25,9},{2,18},{18... | collective-permute-start | bytes 196616 | tf_op jit(solution)/shard_map/ppermute | solution.py:19
  40.1 11.2 %collective-permute-start.2 = (bf16[128,256]{0,1:T(8,128)(2,1)S(1)}, bf16[128,256]{0,1:T(8,128)(2,1)S(1)}, u32[]{:S(2)}, u32[]{:S(2)}) collective-permute-start(bf16[128,256]{0,1:T(8,128)(2,1)S(1)} %add_convert_fusion.4), channel_id=1, source_target_pairs={{0,2},{2,0},{1,3},{3,1},{4,6},{6,4},{5,7},{7,5},{8,10},{10,8},{9,1... | collective-permute-start | bytes 196616 | tf_op jit(solution)/shard_map/ppermute | solution.py:19
  41.7 8.5 %collective-permute-start.4 = (bf16[128,256]{1,0:T(8,128)(2,1)S(1)}, bf16[128,256]{1,0:T(8,128)(2,1)S(1)}, u32[]{:S(2)}, u32[]{:S(2)}) collective-permute-start(bf16[128,256]{1,0:T(8,128)(2,1)S(1)} %add_convert_fusion.3), channel_id=1, source_target_pairs={{0,4},{4,0},{1,5},{5,1},{2,6},{6,2},{3,7},{7,3},{8,12},{12,8},{9,1... | collective-permute-start | bytes 196616 | tf_op jit(solution)/shard_map/ppermute | solution.py:19
  44.9 4.3 %collective-permute-start.6 = (bf16[128,256]{1,0:T(8,128)(2,1)S(1)}, bf16[128,256]{1,0:T(8,128)(2,1)S(1)}, u32[]{:S(2)}, u32[]{:S(2)}) collective-permute-start(bf16[128,256]{1,0:T(8,128)(2,1)S(1)} %add_convert_fusion.2), channel_id=1, source_target_pairs={{0,8},{8,0},{16,24},{24,16},{1,9},{9,1},{17,25},{25,17},{2,10},{10... | collective-permute-start | bytes 196616 | tf_op jit(solution)/shard_map/ppermute | solution.py:19
  56.0 7.8 %copy-start.1 = (bf16[1536,256]{1,0:T(8,128)(2,1)S(1)}, bf16[1536,256]{1,0:T(8,128)(2,1)}, u32[]{:S(2)}) copy-start(bf16[1536,256]{1,0:T(8,128)(2,1)} %param.10) | copy-start | bytes 2359300
  64.1 1.1 copy-start.2
  66.3 100.6 %all-reduce.7.cloned.1.call-start = ((), (), s32[]{:S(2)}) async-start(), calls=%async_computation.1 | async-start | bytes 1048576 | tf_op jit(solution)/shard_map/psum | solution.py:9
Sparse Core Ops, SparseCore 0:
  66.5 52.9 all-reduce.4
  122.4 44.4 all-reduce.6
